TPU v7x, 256 devices: a whole 4x4x8 slice. The times are simulated.
256 devices in a mesh: xy: 32 (over z, x_lo, core), gz: 8 (over y, x_hi).
Axes of the slice: x: 4 (x_hi: 2, x_lo: 2; x = x_hi * 2 + x_lo), y: 4, z: 8, core: 2. Of those that a mesh axis runs over, the one named last changes fastest.
Arguments:
- file_data: float32 [512, 64, 8192], P('gz', None, 'xy')
- factor: float32 [512, 256], P('gz'), may hold values from -0.25 to 0.25
- block_owner: int32 [64], replicated, may hold values from 0 to 31, as said below
- block_offset: int32 [64], replicated, may hold values from 0 to 128, as said below
Outputs:
- gram: float32 [512, 512], P('gz')
- core: float32 [256, 64, 8192], P('gz', None, 'xy')
Inputs may be any that keep to these rules, and one draw needn't show every extreme that they name: `block_owner`: block b of device d (b = d * 2 + j) is owned by d - 1, d or d + 1 modulo 32. Every index of xy owns exactly 2 blocks. `block_offset`: offsets are multiples of 128; the blocks of one owner take distinct offsets, so every file slot is named once.
All inputs are finite; a program needn't handle non-finite values.
Results may differ from a plain program's by a relative error of at most 0.00007.
Values sent between devices are 32-bit elements; how exact they have to be, the bound alone decides.
A program may use at most 128 MiB of HBM per device.

v0:
```python
import jax
import jax.numpy as jnp
from jax import lax
from jax.sharding import PartitionSpec as P

BLOCKS_DEV = 2


def shifted(array, axis, by):
    length = lax.axis_size(axis)
    return lax.ppermute(array, axis, [(i, (i + by) % length) for i in range(length)])


def split_up(array, dim, length):
    shape = array.shape
    tiles = array.reshape(*shape[:dim], length, shape[dim] // length, *shape[dim + 1 :])
    return jnp.moveaxis(tiles, dim, 0)


def sent_and_summed(array, axis, dim):
    length = lax.axis_size(axis)
    tiles = lax.all_to_all(split_up(array, dim, length), axis, 0, 0, tiled=True)
    return jnp.sum(tiles, axis=0)


def over_pieces(array, axis):
    tiles = lax.all_gather(array, axis)
    return tiles.sum(axis=0)


def sent_to_all(array, axis):
    length = lax.axis_size(axis)
    return lax.all_to_all(
        jnp.broadcast_to(array[None], (length, *array.shape)), axis, 0, 0, tiled=True
    )


def joined_along(tiles, dim):
    tiles = jnp.moveaxis(tiles, 0, dim)
    shape = tiles.shape
    return tiles.reshape(*shape[:dim], shape[dim] * shape[dim + 1], *shape[dim + 2 :])


def gather_directly(array, axis, dim):
    tiles = sent_to_all(array, axis)
    return joined_along(tiles, dim)


def take_block(buffer, offset):
    return lax.dynamic_slice_in_dim(buffer, offset, 128, 2)


def rebalance(buffer, block_owner, block_offset):
    devices = lax.axis_size("xy")
    myself = lax.axis_index("xy")
    lower_peer = (myself + devices - 1) % devices
    upper_peer = (myself + 1) % devices
    blank = jnp.zeros(buffer.shape[:2] + (128,), buffer.dtype)

    def outgoing(target):
        pieces = []
        for j in range(BLOCKS_DEV):
            owner = block_owner[target * BLOCKS_DEV + j]
            offset = block_offset[target * BLOCKS_DEV + j]
            pieces.append(jnp.where(owner == myself, take_block(buffer, offset), blank))
        return jnp.concatenate(pieces, axis=2)

    from_lower = shifted(outgoing(upper_peer), "xy", 1)
    from_upper = shifted(outgoing(lower_peer), "xy", -1)
    blocks = []
    for j in range(BLOCKS_DEV):
        owner = block_owner[myself * BLOCKS_DEV + j]
        offset = block_offset[myself * BLOCKS_DEV + j]
        local_block = take_block(buffer, offset)
        lower_block = from_lower[:, :, j * 128 : (j + 1) * 128]
        upper_block = from_upper[:, :, j * 128 : (j + 1) * 128]
        remote = jnp.where(owner == lower_peer, lower_block, upper_block)
        blocks.append(jnp.where(owner == myself, local_block, remote))
    return jnp.concatenate(blocks, axis=2)


def used_slots(file_data, block_owner, block_offset):
    myself = lax.axis_index("xy")
    slot_count = file_data.shape[2] // 128
    hits = (block_owner[:, None] == myself) & (
        block_offset[:, None] // 128 == jnp.arange(slot_count, dtype=jnp.int32)[None, :]
    )
    used = jnp.any(hits, axis=0).astype(jnp.float32)
    return jnp.repeat(used, 128)


def local(file_data, factor, block_owner, block_offset):
    working = file_data * used_slots(file_data, block_owner, block_offset)[None, None, :]
    swapped = lax.all_to_all(working, "gz", split_axis=1, concat_axis=0, tiled=True)
    scale = 1.0 / (BLOCKS_DEV * 128 * lax.axis_size("xy") * file_data.shape[1])
    partial_gram = (
        jnp.einsum("zcs,wcs->zw", swapped, swapped, precision=lax.Precision.HIGHEST) * scale
    )
    gram_block = sent_and_summed(partial_gram, "gz", 0)
    gram = over_pieces(gram_block, "xy")
    whole_factor = gather_directly(factor, "gz", 0)
    core_part = jnp.einsum("zr,zcs->rcs", whole_factor, swapped, precision=lax.Precision.HIGHEST)
    core = lax.all_to_all(core_part, "gz", split_axis=0, concat_axis=1, tiled=True)
    core = rebalance(core, block_owner, block_offset)
    return (gram, core)


def solution(mesh):
    return jax.shard_map(
        local,
        mesh=mesh,
        in_specs=(P("gz", None, "xy"), P("gz", None), P(), P()),
        out_specs=(P("gz", None), P("gz", None, "xy")),
        check_vma=False,
    )
```

profile of v0, /device:TPU:1, one launch (start us, length us, event | category | flops | bytes accessed | tf_op | source)
XLA Modules:
  0.0 235.7 jit_solution(13166197315982324203)
XLA Ops:
  7.2 0.0 all-gather.3.cloned.1.call-start
  7.2 0.7 and_select_fusion
  7.9 0.7 broadcast_compare_fusion
  8.5 0.1 and_reduce_fusion
  8.7 0.1 broadcast_bitcast_fusion
  8.7 4.6 %copy_multiply_fusion = f32[64,64,256]{2,0,1:T(8,128)S(1)} fusion(f32[64,64,256]{2,1,0:T(8,128)} %param.4, f32[256]{0:T(256)S(1)} %broadcast_bitcast_fusion), kind=kLoop, calls=%fused_computation.2 | loop fusion | flops 1048576 | bytes 8389632 | tf_op jit(solution)/shard_map/mul | solution.py:93
  13.4 57.3 %all_to_all.46 = f32[64,64,256]{2,0,1:T(8,128)S(1)} all-to-all(f32[64,64,256]{2,0,1:T(8,128)S(1)} %copy_multiply_fusion), channel_id=1, replica_groups=mesh['xy'=32,'gz'=8] {'gz'}, dimensions={1} | all-to-all | bytes 8388608 | tf_op jit(solution)/shard_map/all_to_all | solution.py:94
  70.7 0.0 copy-start
  70.7 0.5 copy.19
  71.2 1.5 copy-done
  72.7 6.9 %fusion.5 = f32[512,512]{1,0:T(8,128)S(1)} fusion(f32[512,8,256]{2,0,1:T(8,128)S(1)} %bitcast.44), kind=kOutput, calls=%fused_computation.9 | convolution fusion | flops 6442713088 | bytes 5242880 | tf_op jit(solution)/shard_map/zcs,wcs->zw/dot_general | solution.py:97
  79.6 0.0 copy-start.2
  79.6 18.5 %all_to_all.47 = f32[8,64,512]{2,1,0:T(8,128)S(1)} all-to-all(f32[8,64,512]{2,1,0:T(8,128)S(1)} %bitcast.50), channel_id=1, replica_groups=mesh['xy'=32,'gz'=8] {'gz'}, dimensions={0} | all-to-all | bytes 2097152 | tf_op jit(solution)/shard_map/all_to_all | solution.py:22
  98.1 0.7 reduce_sum.18
  98.8 0.0 all-gather.3.cloned.1.call-update
  98.8 0.0 copy-done.2
  98.9 11.5 %all_to_all.48 = f32[8,64,256]{2,1,0:T(8,128)S(1)} all-to-all(f32[8,64,256]{2,1,0:T(8,128)S(1)} %broadcast_in_dim.7), channel_id=1, replica_groups=mesh['xy'=32,'gz'=8] {'gz'}, dimensions={0} | all-to-all | bytes 1048576 | tf_op jit(solution)/shard_map/all_to_all | solution.py:33
  110.3 8.6 %fusion.2 = f32[256,8,256]{0,2,1:T(8,128)S(1)} fusion(f32[8,64,256]{2,1,0:T(8,128)S(1)} %all_to_all.48, f32[64,8,8,256]{3,0,2,1:T(8,128)} %bitcast.48), kind=kOutput, calls=%fused_computation.7 | convolution fusion | flops 3221225472 | bytes 6815744 | tf_op jit(solution)/shard_map/zr,zcs->rcs/dot_general | solution.py:102
  118.9 2.0 copy.20
  120.9 0.0 copy-start.3
  120.9 0.0 copy-start.4
  120.9 3.7 %all-to-all-start.3 = ((f32[256,8,256]{2,1,0:T(8,128)}), f32[256,8,256]{2,1,0:T(8,128)S(1)}, u32[]{:S(2)}, u32[]{:S(2)}) async-start(f32[256,8,256]{2,1,0:T(8,128)} %copy.20), calls=%async_computation.3 | async-start | bytes 4194304 | tf_op jit(solution)/shard_map/all_to_all | solution.py:103
  124.7 0.0 copy-done.3
  124.7 0.0 copy-done.4
  124.7 0.7 fusion.10
  135.7 29.0 %all-to-all-done.3 = f32[256,8,256]{2,1,0:T(8,128)S(1)} async-done(((f32[256,8,256]{2,1,0:T(8,128)}), f32[256,8,256]{2,1,0:T(8,128)S(1)}, u32[]{:S(2)}, u32[]{:S(2)}) %all-to-all-start.3) | async-done | bytes 2097184 | tf_op jit(solution)/shard_map/all_to_all | solution.py:103
  164.7 0.0 copy-start.1
  164.7 1.3 copy-done.1
  166.0 1.9 copy.31
  167.9 1.2 dynamic-slice_select_fusion.3
  169.1 1.5 pad_maximum_fusion.1
  170.5 3.9 %collective-permute-start.1 = (f32[32,64,256]{2,1,0:T(8,128)}, f32[32,64,256]{2,1,0:T(8,128)}, u32[]{:S(2)}, u32[]{:S(2)}) collective-permute-start(f32[32,64,256]{2,1,0:T(8,128)} %pad_maximum_fusion.1), channel_id=1, source_target_pairs={{0,248},{8,0},{16,8},{24,16},{32,24},{40,32},{48,40},{56,48},{64,5... | collective-permute-start | bytes 6291464 | tf_op jit(solution)/shard_map/ppermute | solution.py:11
  174.5 1.5 pad_maximum_fusion
  176.0 0.3 collective-permute-start
  182.3 38.9 %collective-permute-done.1 = f32[32,64,256]{2,1,0:T(8,128)} collective-permute-done((f32[32,64,256]{2,1,0:T(8,128)}, f32[32,64,256]{2,1,0:T(8,128)}, u32[]{:S(2)}, u32[]{:S(2)}) %collective-permute-start.1) | collective-permute-done | bytes 2097184 | tf_op jit(solution)/shard_map/ppermute | solution.py:11
  221.3 0.0 collective-permute-done
  221.3 2.9 %fusion.7 = (f32[32,64,128]{2,1,0:T(8,128)S(1)}, f32[32,64,128]{2,1,0:T(8,128)S(1)}) fusion(f32[32,64,256]{2,1,0:T(8,128)} %collective-permute-done.1, f32[32,64,256]{2,1,0:T(8,128)} %collective-permute-done, f32[32,64,256]{2,1,0:T(8,128)S(1)} %bitcast.46, s32[]{:T(128)S(6)} %select_n.112, pred[]{:T(512)S(6)} %eq.53, pred[]{:T(512)S(6)} %eq.52, pred[]{:T(512)S(6)} %eq.59, ...), kind=kLoop, calls=%fused_computation.13 | loop fusion | flops 1048576 | bytes 8388620 | tf_op jit(solution)/shard_map/jit(_where)/select_n | solution.py:78
  224.2 1.5 pad_maximum_fusion.2
  225.7 0.0 all-gather.3.cloned.1.call-done
  225.7 3.2 %reduce_sum.19 = f32[64,512]{1,0:T(8,128)} reduce(f32[32,64,512]{2,1,0:T(8,128)} %bitcast.51, f32[]{:T(128)} %constant.52.clone.1), dimensions={0}, to_apply=%region_2.3 | reduce | flops 1015808 | bytes 4325380 | tf_op jit(solution)/shard_map/reduce_sum | solution.py:28
  (2 shorter events, 0.0 us)
Async XLA Ops:
  7.2 218.5 %all-gather.3.cloned.1.call-start = ((), (), s32[]{:S(2)}) async-start(), calls=%async_computation.4 | async-start | bytes 4325376 | tf_op jit(solution)/shard_map/all_gather | solution.py:27
  70.7 2.0 copy-start
  79.6 19.2 %copy-start.2 = (f32[64,256]{1,0:T(8,128)S(1)}, f32[64,256]{1,0:T(8,128)}, u32[]{:S(2)}) copy-start(f32[64,256]{1,0:T(8,128)} %param.5) | copy-start | bytes 196612
  120.9 3.8 %copy-start.3 = (s32[64]{0:T(128)S(1)}, s32[64]{0:T(128)}, u32[]{:S(2)}) copy-start(s32[64]{0:T(128)} %param.6) | copy-start | bytes 772
  120.9 3.8 %copy-start.4 = (s32[64]{0:T(128)S(1)}, s32[64]{0:T(128)}, u32[]{:S(2)}) copy-start(s32[64]{0:T(128)} %param.7) | copy-start | bytes 772
  120.9 43.8 %all-to-all-start.3 = ((f32[256,8,256]{2,1,0:T(8,128)}), f32[256,8,256]{2,1,0:T(8,128)S(1)}, u32[]{:S(2)}, u32[]{:S(2)}) async-start(f32[256,8,256]{2,1,0:T(8,128)} %copy.20), calls=%async_computation.3 | async-start | bytes 4194304 | tf_op jit(solution)/shard_map/all_to_all | solution.py:103
  164.7 1.3 copy-start.1
  170.5 50.7 %collective-permute-start.1 = (f32[32,64,256]{2,1,0:T(8,128)}, f32[32,64,256]{2,1,0:T(8,128)}, u32[]{:S(2)}, u32[]{:S(2)}) collective-permute-start(f32[32,64,256]{2,1,0:T(8,128)} %pad_maximum_fusion.1), channel_id=1, source_target_pairs={{0,248},{8,0},{16,8},{24,16},{32,24},{40,32},{48,40},{56,48},{64,5... | collective-permute-start | bytes 6291464 | tf_op jit(solution)/shard_map/ppermute | solution.py:11
  176.0 45.3 %collective-permute-start = (f32[32,64,256]{2,1,0:T(8,128)}, f32[32,64,256]{2,1,0:T(8,128)}, u32[]{:S(2)}, u32[]{:S(2)}) collective-permute-start(f32[32,64,256]{2,1,0:T(8,128)} %pad_maximum_fusion), channel_id=1, source_target_pairs={{0,8},{8,16},{16,24},{24,32},{32,40},{40,48},{48,56},{56,64},{64,7... | collective-permute-start | bytes 6291464 | tf_op jit(solution)/shard_map/ppermute | solution.py:11
Sparse Core Ops, SparseCore 0:
  98.9 67.6 all-gather.2
where the time goes:
time: 236 us
  blocking collectives  87.3 us (37%)
  waiting for transfers between devices  68 us (29%)
  between operations  30.5 us (13%)
  other arithmetic  18.6 us (8%)
  matrix products  15.5 us (7%)
  starting transfers between devices  8 us (3%)
  local copies, waits for them, and re-layouts  7.97 us (3%)
    all_to_all x1, blocking collectives, local(): lax.all_to_all(working, 'gz', split_axis=1, concat_axis=0, tiled=True)  57.3 us
    ppermute x2, waiting for transfers between devices, shifted(): lax.ppermute(array, axis, [(i, (i + by) % length) for i in range(length)])  38.9 us
    all_to_all x1, waiting for transfers between devices, local(): lax.all_to_all(core_part, 'gz', split_axis=0, concat_axis=1, tiled=True)  29 us
    all_to_all x1, blocking collectives, sent_and_summed(): tiles = lax.all_to_all(split_up(array, dim, length), axis, 0, 0, tiled=True)  18.5 us
    all_to_all x1, blocking collectives, sent_to_all(): lax.all_to_all(jnp.broadcast_to(array[None], (length, *array.shape)), axi...  11.5 us
    dot_general x1, matrix products, local(): jnp.einsum('zr,zcs->rcs', whole_factor, swapped, precision=lax.Precision....  8.57 us
    dot_general x1, matrix products, local(): jnp.einsum('zcs,wcs->zw', swapped, swapped, precision=lax.Precision.HIGHEST)  6.89 us
  transfers between devices with their start and end apart: 4, of which 2 were waited for; matrix products, arithmetic and copies ran while one was open for 9% of the time, Pallas kernels for 0%

commit v1 on v0

v1 whole, which is shorter than its diff:
```python
import jax
import jax.numpy as jnp
from jax import lax
from jax.sharding import PartitionSpec as P

BLOCKS_DEV = 2


def shifted(array, axis, by):
    length = lax.axis_size(axis)
    return lax.ppermute(array, axis, [(i, (i + by) % length) for i in range(length)])


def take_block(buffer, offset):
    return lax.dynamic_slice_in_dim(buffer, offset, 128, 2)


def rebalance(buffer, block_owner, block_offset):
    devices = lax.axis_size("xy")
    myself = lax.axis_index("xy")
    lower_peer = (myself + devices - 1) % devices
    upper_peer = (myself + 1) % devices

    def outgoing(target):
        pieces = []
        for j in range(BLOCKS_DEV):
            pieces.append(take_block(buffer, block_offset[target * BLOCKS_DEV + j]))
        return jnp.concatenate(pieces, axis=2)

    from_lower = shifted(outgoing(upper_peer), "xy", 1)
    from_upper = shifted(outgoing(lower_peer), "xy", -1)
    blocks = []
    for j in range(BLOCKS_DEV):
        owner = block_owner[myself * BLOCKS_DEV + j]
        offset = block_offset[myself * BLOCKS_DEV + j]
        local_block = take_block(buffer, offset)
        lower_block = from_lower[:, :, j * 128 : (j + 1) * 128]
        upper_block = from_upper[:, :, j * 128 : (j + 1) * 128]
        remote = jnp.where(owner == lower_peer, lower_block, upper_block)
        blocks.append(jnp.where(owner == myself, local_block, remote))
    return jnp.concatenate(blocks, axis=2)


def halves(x):
    high = lax.reduce_precision(x, exponent_bits=8, mantissa_bits=7)
    low = x - high
    return high.astype(jnp.bfloat16), low.astype(jnp.bfloat16)


def dot(spec, a, b):
    return jnp.einsum(spec, a, b, preferred_element_type=jnp.float32)


def local(file_data, factor, block_owner, block_offset):
    whole_factor = lax.all_gather(factor, "gz", axis=0, tiled=True)
    swapped = lax.all_to_all(file_data, "gz", split_axis=1, concat_axis=0, tiled=True)
    scale = 1.0 / (BLOCKS_DEV * 128 * lax.axis_size("xy") * file_data.shape[1])
    high, low = halves(swapped)
    factor_high, factor_low = halves(whole_factor)
    core_part = (
        dot("zr,zcs->rcs", factor_high, high)
        + dot("zr,zcs->rcs", factor_high, low)
        + dot("zr,zcs->rcs", factor_low, high)
    )
    core = lax.all_to_all(core_part, "gz", split_axis=0, concat_axis=1, tiled=True)
    cross = dot("zcs,wcs->zw", high, low)
    partial_gram = (dot("zcs,wcs->zw", high, high) + (cross + cross.T)) * scale
    gram = lax.psum_scatter(partial_gram, "gz", scatter_dimension=0, tiled=True)
    gram = lax.psum(gram, "xy")
    core = rebalance(core, block_owner, block_offset)
    return (gram, core)


def solution(mesh):
    return jax.shard_map(
        local,
        mesh=mesh,
        in_specs=(P("gz", None, "xy"), P("gz", None), P(), P()),
        out_specs=(P("gz", None), P("gz", None, "xy")),
        check_vma=False,
    )
```

time: 236 us -> 450 us (1.91)
  waiting for transfers between devices: 68 us -> 287 us
  blocking collectives: 87.3 us -> 73.6 us
  local copies, waits for them, and re-layouts: 7.97 us -> 21.1 us
  starting transfers between devices: 8 us -> 19.9 us
  matrix products: 15.5 us -> 8.24 us
  other arithmetic: 18.6 us -> 11.6 us
    psum x0 -> x1, waiting for transfers between devices: none -> 203 us  [local(): gram = lax.psum(gram, 'xy')]
    all_to_all x3 -> x0, blocking collectives: 87.3 us -> none  [the longest x1 57.3 us: local(): lax.all_to_all(working, 'gz', split_axis=1, concat_axis=0, tiled=True)]
    reduce_scatter x0 -> x1, waiting for transfers between devices: none -> 82.5 us  [local(): gram = lax.psum_scatter(partial_gram, 'gz', scatter_dimension=0, tiled=True)]
    all_gather x0 -> x1, blocking collectives: none -> 73.6 us  [local(): whole_factor = lax.all_gather(factor, 'gz', axis=0, tiled=True)]
    ppermute x2, waiting for transfers between devices: 38.9 us -> 0.01 us  [shifted(): lax.ppermute(array, axis, [(i, (i + by) % length) for i in range(length)])]
    all_to_all x1, waiting for transfers between devices: 29 us -> 1.04 us  [local(): lax.all_to_all(core_part, 'gz', split_axis=0, concat_axis=1, tiled=True)]
    unnamed x10 -> x12, local copies, waits for them, and re-layouts: 2.84 us -> 10.8 us
    all_to_all x0 -> x1, starting transfers between devices: none -> 7.6 us  [local(): lax.all_to_all(file_data, 'gz', split_axis=1, concat_axis=0, tiled=True)]
  transfers between devices with their start and end apart: 4 -> 6, of which waited for: 2 -> 3; matrix products, arithmetic and copies ran while one was open for 9% -> 5% of each run, Pallas kernels for 0% -> 0%
where the time goes in v1:
time: 450 us; the launch traced here: 449 us
  waiting for transfers between devices  287 us (64%)
  blocking collectives  73.6 us (16%)
  between operations  28 us (6%)
  local copies, waits for them, and re-layouts  21.1 us (5%)
  starting transfers between devices  19.9 us (4%)
  other arithmetic  11.6 us (3%)
  matrix products  8.24 us (2%)
    psum x1, waiting for transfers between devices, local(): gram = lax.psum(gram, 'xy')  203 us
    reduce_scatter x1, waiting for transfers between devices, local(): gram = lax.psum_scatter(partial_gram, 'gz', scatter_dimension=0, tiled=True)  82.5 us
    all_gather x1, blocking collectives, local(): whole_factor = lax.all_gather(factor, 'gz', axis=0, tiled=True)  73.6 us
    unnamed x12, local copies, waits for them, and re-layouts  10.8 us
  transfers between devices with their start and end apart: 6, of which 3 were waited for; matrix products, arithmetic and copies ran while one was open for 5% of the time, Pallas kernels for 0%

profile of v1, /device:TPU:1, one launch (start us, length us, event | category | flops | bytes accessed | tf_op | source)
XLA Modules:
  0.0 449.3 jit_solution(16877087336601075316)
XLA Ops:
  7.2 6.6 %copy.13 = f32[64,64,256]{2,0,1:T(8,128)} copy(f32[64,64,256]{2,1,0:T(8,128)} %param.4) | data formatting | bytes 8388608 | tf_op args[0]
  13.8 0.0 copy-start.2
  13.8 7.6 %all-to-all-start = ((f32[64,64,256]{2,0,1:T(8,128)}), f32[64,64,256]{2,0,1:T(8,128)}, u32[]{:S(2)}, u32[]{:S(2)}) async-start(f32[64,64,256]{2,0,1:T(8,128)} %copy.13), calls=%async_computation | async-start | bytes 8388608 | tf_op jit(solution)/shard_map/all_to_all | solution.py:56
  21.4 0.0 copy-done.2
  21.4 73.6 %all_gather.3 = f32[512,256]{1,0:T(8,128)S(1)} all-gather(f32[64,256]{1,0:T(8,128)S(1)} %copy-done.2), channel_id=1, replica_groups=mesh['xy'=32,'gz'=8] {'gz'}, dimensions={0}, use_global_device_ids=true | all-gather | bytes 589824 | tf_op jit(solution)/shard_map/all_gather | solution.py:55
  94.9 0.2 copy.16
  95.1 0.0 all-to-all-done
  95.1 2.5 copy.14
  97.6 1.0 fusion.1
  98.6 0.7 fusion.9
  99.4 0.7 fusion.13
  100.1 0.8 fusion.2
  100.9 2.6 copy.21
  103.4 0.0 copy-start.3
  103.4 0.0 copy-start.4
  103.5 3.7 all-to-all-start.1
  107.2 0.0 reduce-scatter.2.cloned.1.call-start
  107.3 0.0 copy-done.3
  107.3 0.0 copy-done.4
  107.3 0.7 fusion.15
  115.4 3.1 fusion
  118.6 0.0 copy-start.1
  118.6 1.3 copy-done.1
  119.9 1.3 convolution_bitcast_fusion
  121.2 1.3 copy.15
  122.5 4.8 %fusion.4 = f32[512,512]{1,0:T(8,128)} fusion(bf16[512,8,256]{2,0,1:T(8,128)(2,1)} %bitcast.59, f32[512,512]{1,0:T(8,128)S(1)} %convolution_bitcast_fusion, f32[512,512]{0,1:T(8,128)} %copy.15), kind=kOutput, calls=%fused_computation.15 | convolution fusion | flops 1074528256 | bytes 5242880 | tf_op jit(solution)/shard_map/zcs,wcs->zw/dot_general | solution.py:51
  127.3 0.0 reduce-scatter.2.cloned.1.call-update
  127.3 0.0 all-reduce.2.cloned.1.call-start
  127.3 1.0 all-to-all-done.1
  128.4 0.0 copy-start
  128.4 1.3 copy-done
  129.7 1.9 copy.30
  131.6 1.2 constant_dynamic-slice_fusion.3
  132.7 1.5 pad_maximum_fusion.1
  134.2 8.2 %collective-permute-start.1 = (f32[32,64,256]{2,1,0:T(8,128)}, f32[32,64,256]{2,1,0:T(8,128)}, u32[]{:S(2)}, u32[]{:S(2)}) collective-permute-start(f32[32,64,256]{2,1,0:T(8,128)} %pad_maximum_fusion.1), channel_id=1, source_target_pairs={{0,248},{8,0},{16,8},{24,16},{32,24},{40,32},{48,40},{56,48},{64,5... | collective-permute-start | bytes 6291464 | tf_op jit(solution)/shard_map/ppermute | solution.py:11
  142.5 1.5 pad_maximum_fusion
  144.0 0.2 collective-permute-start
  150.5 82.5 %reduce-scatter.2.cloned.1.call-done = f32[64,512]{1,0:T(8,128)} async-done(((f32[512,512]{1,0:T(8,128)}), f32[64,512]{1,0:T(8,128)}) %reduce-scatter.2.cloned.1.call-update) | async-done | bytes 131088 | tf_op jit(solution)/shard_map/reduce_scatter | solution.py:68
  233.0 0.0 all-reduce.2.cloned.1.call-update
  233.0 0.0 collective-permute-done.1
  233.0 0.0 collective-permute-done
  233.0 2.9 fusion.6
  236.0 1.5 pad_maximum_fusion.2
  237.5 203.4 %all-reduce.2.cloned.1.call-done = f32[64,512]{1,0:T(8,128)} async-done(((f32[64,512]{1,0:T(8,128)}), f32[64,512]{1,0:T(8,128)}) %all-reduce.2.cloned.1.call-update) | async-done | bytes 131088 | tf_op jit(solution)/shard_map/psum | solution.py:69
  440.9 1.6 copy.32
Async XLA Ops:
  13.8 7.6 %copy-start.2 = (f32[64,256]{1,0:T(8,128)S(1)}, f32[64,256]{1,0:T(8,128)}, u32[]{:S(2)}) copy-start(f32[64,256]{1,0:T(8,128)} %param.5) | copy-start | bytes 196612
  13.8 81.4 %all-to-all-start = ((f32[64,64,256]{2,0,1:T(8,128)}), f32[64,64,256]{2,0,1:T(8,128)}, u32[]{:S(2)}, u32[]{:S(2)}) async-start(f32[64,64,256]{2,0,1:T(8,128)} %copy.13), calls=%async_computation | async-start | bytes 8388608 | tf_op jit(solution)/shard_map/all_to_all | solution.py:56
  103.4 3.8 copy-start.3
  103.4 3.8 copy-start.4
  103.5 24.9 %all-to-all-start.1 = ((f32[256,8,256]{2,1,0:T(8,128)}), f32[256,8,256]{2,1,0:T(8,128)S(1)}, u32[]{:S(2)}, u32[]{:S(2)}) async-start(f32[256,8,256]{2,1,0:T(8,128)} %copy.21), calls=%async_computation.2 | async-start | bytes 4194304 | tf_op jit(solution)/shard_map/all_to_all | solution.py:65
  107.2 125.8 %reduce-scatter.2.cloned.1.call-start = ((), (), s32[]{:S(2)}) async-start(), calls=%async_computation.3 | async-start | bytes 1179648 | tf_op jit(solution)/shard_map/reduce_scatter | solution.py:68
  118.6 1.3 copy-start.1
  127.3 313.6 %all-reduce.2.cloned.1.call-start = ((), (), s32[]{:S(2)}) async-start(), calls=%async_computation.4 | async-start | bytes 262144 | tf_op jit(solution)/shard_map/psum | solution.py:69
  128.4 1.3 copy-start
  134.2 98.8 %collective-permute-start.1 = (f32[32,64,256]{2,1,0:T(8,128)}, f32[32,64,256]{2,1,0:T(8,128)}, u32[]{:S(2)}, u32[]{:S(2)}) collective-permute-start(f32[32,64,256]{2,1,0:T(8,128)} %pad_maximum_fusion.1), channel_id=1, source_target_pairs={{0,248},{8,0},{16,8},{24,16},{32,24},{40,32},{48,40},{56,48},{64,5... | collective-permute-start | bytes 6291464 | tf_op jit(solution)/shard_map/ppermute | solution.py:11
  144.0 89.1 %collective-permute-start = (f32[32,64,256]{2,1,0:T(8,128)}, f32[32,64,256]{2,1,0:T(8,128)}, u32[]{:S(2)}, u32[]{:S(2)}) collective-permute-start(f32[32,64,256]{2,1,0:T(8,128)} %pad_maximum_fusion), channel_id=1, source_target_pairs={{0,8},{8,16},{16,24},{24,32},{32,40},{40,48},{48,56},{56,64},{64,7... | collective-permute-start | bytes 6291464 | tf_op jit(solution)/shard_map/ppermute | solution.py:11
Sparse Core Ops, SparseCore 0:
  127.4 105.5 reduce-scatter.1
  235.6 205.2 all-reduce.1

commit v2 on v1

v2 whole, which is shorter than its diff:
```python
import functools

import jax
import jax.numpy as jnp
from jax import lax
from jax.experimental import pallas as pl
from jax.experimental.pallas import tpu as pltpu
from jax.sharding import PartitionSpec as P

MESH = pl.DeviceIdType.MESH
GZ = 8
LANES = 128
SWAP_ORDER = (4, 1, 6, 2, 7, 5, 3)
SCATTER_ORDER = (
    (6, 1), (0, 0), (5, 0), (3, 0), (2, 0), (4, 1), (4, 0), (1, 0),
    (5, 1), (2, 1), (3, 1), (7, 1), (1, 1), (7, 0), (6, 0),
)


def mirrored(offset):
    return (4 - offset // 2) % 4 * 2 + offset % 2


def place():
    d = lax.axis_index("xy")
    g = lax.axis_index("gz")
    return d, g, lax.rem(d, 2)


def by_core(core, offset):
    other = mirrored(offset)
    return offset if offset == other else offset * (1 - core) + other * core


def peer(g, offset):
    if isinstance(offset, int):
        dy, dx = offset // 2, offset % 2
    else:
        dy, dx = lax.div(offset, 2), lax.rem(offset, 2)
    return lax.rem(lax.div(g, 2) + dy, 4) * 2 + lax.rem(lax.rem(g, 2) + dx, 2)


def greet(peers):
    barrier = pltpu.get_barrier_semaphore()
    for where in peers:
        pl.semaphore_signal(barrier, inc=1, device_id=where, device_id_type=MESH)
    pl.semaphore_wait(barrier, len(peers))


def swap_kernel(x_ref, f_ref, out_ref, factor_ref, local_sem, x_send, x_recv, f_send, f_recv):
    d, g, core = place()
    greet([{"xy": d, "gz": peer(g, o)} for o in range(1, GZ)])
    copies = []
    for step in SWAP_ORDER:
        o = by_core(core, step)
        to = peer(g, o)
        copies.append(
            pltpu.make_async_remote_copy(
                src_ref=x_ref.at[:, pl.ds(pl.multiple_of(to * 8, 8), 8), :],
                dst_ref=out_ref.at[g],
                send_sem=x_send.at[o],
                recv_sem=x_recv.at[o],
                device_id={"xy": d, "gz": to},
                device_id_type=MESH,
            )
        )
        copies.append(
            pltpu.make_async_remote_copy(
                src_ref=f_ref,
                dst_ref=factor_ref.at[g],
                send_sem=f_send.at[o],
                recv_sem=f_recv.at[o],
                device_id={"xy": d, "gz": to},
                device_id_type=MESH,
            )
        )
    for copy in copies:
        copy.start()
    mine = x_ref.at[:, pl.ds(pl.multiple_of(g * 8, 8), 8), :]
    own = pltpu.make_async_copy(mine, out_ref.at[g], local_sem.at[0])
    own_factor = pltpu.make_async_copy(f_ref, factor_ref.at[g], local_sem.at[1])
    own.start()
    own_factor.start()
    own.wait()
    own_factor.wait()
    for copy in copies:
        copy.wait()


def swap(field, factor):
    planes, species, points = field.shape
    return pl.pallas_call(
        swap_kernel,
        out_shape=(
            jax.ShapeDtypeStruct((GZ, planes, species // GZ, points), jnp.float32),
            jax.ShapeDtypeStruct((GZ, *factor.shape), jnp.float32),
        ),
        in_specs=[pl.BlockSpec(memory_space=pl.ANY)] * 2,
        out_specs=[pl.BlockSpec(memory_space=pltpu.VMEM)] * 2,
        scratch_shapes=[
            pltpu.SemaphoreType.DMA((2,)),
            pltpu.SemaphoreType.DMA((GZ,)),
            pltpu.SemaphoreType.DMA((GZ,)),
            pltpu.SemaphoreType.DMA((GZ,)),
            pltpu.SemaphoreType.DMA((GZ,)),
        ],
        compiler_params=pltpu.CompilerParams(collective_id=0, has_side_effects=True),
        name="swap",
    )(field, factor)


def halves(x):
    high = x.astype(jnp.bfloat16)
    return high, (x - high.astype(jnp.float32)).astype(jnp.bfloat16)


def product_kernel(scale, x_ref, f_ref, gram_ref, core_ref, high_ref, low_ref):
    z = x_ref.shape[0] * x_ref.shape[1]
    species, points = x_ref.shape[2:]
    f_high, f_low = halves(f_ref[...])
    dot = functools.partial(jnp.dot, preferred_element_type=jnp.float32)
    for c in range(species):
        x = x_ref[:, :, c, :].reshape(z, points)
        high, low = halves(x)
        high_ref[:, c * points : (c + 1) * points] = high
        low_ref[:, c * points : (c + 1) * points] = low
        core_ref[c] = dot(f_high, high) + dot(f_high, low) + dot(f_low, high)
    across = (((1,), (1,)), ((), ()))
    high = high_ref[...]
    gram = lax.dot_general(high, high, across, preferred_element_type=jnp.float32)
    cross = lax.dot_general(high, low_ref[...], across, preferred_element_type=jnp.float32)
    gram_ref[...] = (gram + (cross + cross.T)) * scale


def products(swapped, factor_t, scale):
    groups, planes, species, points = swapped.shape
    z, rank = groups * planes, factor_t.shape[0]
    return pl.pallas_call(
        functools.partial(product_kernel, scale),
        out_shape=(
            jax.ShapeDtypeStruct((z, z), jnp.float32),
            jax.ShapeDtypeStruct((species, rank, points), jnp.float32),
        ),
        in_specs=[pl.BlockSpec(memory_space=pltpu.VMEM)] * 2,
        out_specs=[pl.BlockSpec(memory_space=pltpu.VMEM)] * 2,
        scratch_shapes=[
            pltpu.VMEM((z, species * points), jnp.bfloat16),
            pltpu.VMEM((z, species * points), jnp.bfloat16),
        ],
        name="products",
    )(swapped, factor_t)


def scatter_kernel(core_ref, out_ref, local_sem, send, recv, pair_send, pair_recv):
    d, g, core = place()
    beyond = lax.rem(d + 31 + 2 * core, 32)
    pair = d + 1 - 2 * core
    rows = core_ref.shape[1] // GZ

    def part(to):
        return core_ref.at[:, pl.ds(pl.multiple_of(to * rows, rows), rows), :]

    greet(
        [{"xy": d, "gz": peer(g, o)} for o in range(1, GZ)]
        + [{"xy": beyond, "gz": peer(g, o)} for o in range(GZ)]
        + [{"xy": pair, "gz": g}]
    )
    copies = {}
    for step, kind in SCATTER_ORDER:
        o = by_core(core, step)
        to = peer(g, o)
        copies[step, kind] = pltpu.make_async_remote_copy(
            src_ref=part(to),
            dst_ref=out_ref.at[kind, g],
            send_sem=send.at[2 * o + kind],
            recv_sem=recv.at[2 * o + kind],
            device_id={"xy": d if kind else beyond, "gz": to},
            device_id_type=MESH,
        )
        copies[step, kind].start()

    def to_pair(source, slot, src_ref):
        return pltpu.make_async_remote_copy(
            src_ref=src_ref,
            dst_ref=out_ref.at[2, source],
            send_sem=pair_send.at[slot],
            recv_sem=pair_recv.at[slot],
            device_id={"xy": pair, "gz": g},
            device_id_type=MESH,
        )

    passed = [to_pair(g, 0, part(g))]
    passed[0].start()
    own = pltpu.make_async_copy(part(g), out_ref.at[1, g], local_sem)
    own.start()
    for step, kind in SCATTER_ORDER:
        copies[step, kind].wait_recv()
        if kind == 1:
            source = peer(g, by_core(core, mirrored(step)))
            passed.append(to_pair(source, step, out_ref.at[1, source]))
            passed[-1].start()
    own.wait()
    for copy in copies.values():
        copy.wait_send()
    for copy in passed:
        copy.wait()


def scatter(core):
    species, rank, points = core.shape
    return pl.pallas_call(
        scatter_kernel,
        out_shape=jax.ShapeDtypeStruct((3, GZ, species, rank // GZ, points), jnp.float32),
        in_specs=[pl.BlockSpec(memory_space=pltpu.VMEM)],
        out_specs=pl.BlockSpec(memory_space=pl.ANY),
        scratch_shapes=[
            pltpu.SemaphoreType.DMA,
            pltpu.SemaphoreType.DMA((2 * GZ,)),
            pltpu.SemaphoreType.DMA((2 * GZ,)),
            pltpu.SemaphoreType.DMA((GZ,)),
            pltpu.SemaphoreType.DMA((GZ,)),
        ],
        compiler_params=pltpu.CompilerParams(collective_id=1, has_side_effects=True),
        cost_estimate=pl.CostEstimate(flops=0, transcendentals=0, bytes_accessed=200_000_000),
        name="scatter",
    )(core)


def place_kernel(which_ref, half_ref, in_ref, out_ref):
    for c in range(in_ref.shape[2]):
        out_ref[:, c, :] = in_ref[0, 0, c]


def placed(candidates, which, half):
    _, groups, species, rows, points = candidates.shape
    grid_spec = pltpu.PrefetchScalarGridSpec(
        num_scalar_prefetch=2,
        grid=(groups, points // LANES),
        in_specs=[
            pl.BlockSpec(
                (1, 1, species, rows, LANES),
                lambda i, j, which, half: (which[j], i, 0, 0, half[j]),
            )
        ],
        out_specs=pl.BlockSpec((rows, species, LANES), lambda i, j, which, half: (0, i, j)),
    )
    return pl.pallas_call(
        place_kernel,
        out_shape=jax.ShapeDtypeStruct((rows, groups * species, points), jnp.float32),
        grid_spec=grid_spec,
        name="placed",
    )(which, half, candidates)


def local(file_data, factor, block_owner, block_offset):
    myself = lax.axis_index("xy")
    blocks = file_data.shape[2] // LANES
    owner = lax.dynamic_slice_in_dim(block_owner, myself * blocks, blocks)
    half = lax.dynamic_slice_in_dim(block_offset, myself * blocks, blocks) // LANES
    pair = myself + 1 - 2 * (myself % 2)
    which = jnp.where(owner == myself, 1, jnp.where(owner == pair, 2, 0)).astype(jnp.int32)

    swapped, factors = swap(file_data, factor)
    factor_t = factors.reshape(-1, factor.shape[1]).T
    scale = 1.0 / (file_data.shape[2] * lax.axis_size("xy") * file_data.shape[1])
    partial_gram, core_part = products(swapped, factor_t, scale)
    planes = file_data.shape[0]
    tiles = lax.all_to_all(
        partial_gram.reshape(GZ, planes, partial_gram.shape[1]), "gz", 0, 0, tiled=True
    )
    gram = lax.all_gather(jnp.sum(tiles, axis=0), "xy").sum(axis=0)
    core_part, tiles = lax.optimization_barrier((core_part, tiles))
    core = placed(scatter(core_part), which, half)
    return (gram, core)


def solution(mesh):
    return jax.shard_map(
        local,
        mesh=mesh,
        in_specs=(P("gz", None, "xy"), P("gz", None), P(), P()),
        out_specs=(P("gz", None), P("gz", None, "xy")),
        check_vma=False,
    )
```

time: 450 us -> 213 us (0.47)
  waiting for transfers between devices: 287 us -> 0.02 us
  Pallas kernels: 0 us -> 167 us
  blocking collectives: 73.6 us -> 21.3 us
  starting transfers between devices: 19.9 us -> 0.04 us
  local copies, waits for them, and re-layouts: 21.1 us -> 2.07 us
  between operations: 28 us -> 14.1 us
  matrix products: 8.24 us -> 0 us
  other arithmetic: 11.6 us -> 4.54 us
    psum x1 -> x0, waiting for transfers between devices: 203 us -> none  [local(): gram = lax.psum(gram, 'xy')]
    pallas_call x0 -> x4, Pallas kernels: none -> 167 us  [the longest x1 76.7 us: scatter(): pl.pallas_call(scatter_kernel, out_shape=jax.ShapeDtypeStruct((3, GZ, spe...]
    reduce_scatter x1 -> x0, waiting for transfers between devices: 82.5 us -> none  [local(): gram = lax.psum_scatter(partial_gram, 'gz', scatter_dimension=0, tiled=True)]
    all_gather x1 -> x0, blocking collectives: 73.6 us -> none  [local(): whole_factor = lax.all_gather(factor, 'gz', axis=0, tiled=True)]
    all_to_all x0 -> x1, blocking collectives: none -> 21.3 us  [local(): lax.all_to_all(partial_gram.reshape(GZ, planes, partial_gram.shape[1]), '...]
    all_to_all x2 -> x0, starting transfers between devices: 11.3 us -> none  [the longest x1 7.6 us: local(): lax.all_to_all(file_data, 'gz', split_axis=1, concat_axis=0, tiled=True)]
    unnamed x12 -> x4, local copies, waits for them, and re-layouts: 10.8 us -> 0.01 us
    ppermute x2 -> x0, starting transfers between devices: 8.44 us -> none  [shifted(): lax.ppermute(array, axis, [(i, (i + by) % length) for i in range(length)])]
  transfers between devices with their start and end apart: 6 -> 1, of which waited for: 3 -> 0; matrix products, arithmetic and copies ran while one was open for 5% -> 0% of each run, Pallas kernels for 0% -> 42%
where the time goes in v2:
time: 213 us; the launch traced here: 209 us
  Pallas kernels  167 us (78%)
  blocking collectives  21.3 us (10%)
  between operations  14.1 us (7%)
  other arithmetic  4.54 us (2%)
    pallas_call x1, Pallas kernels, scatter(): pl.pallas_call(scatter_kernel, out_shape=jax.ShapeDtypeStruct((3, GZ, spe...  76.7 us
    pallas_call x1, Pallas kernels, swap(): pl.pallas_call(swap_kernel, out_shape=(jax.ShapeDtypeStruct((GZ, planes,...  60.2 us
    all_to_all x1, blocking collectives, local(): lax.all_to_all(partial_gram.reshape(GZ, planes, partial_gram.shape[1]), '...  21.3 us
    pallas_call x1, Pallas kernels, products(): pl.pallas_call(functools.partial(product_kernel, scale), out_shape=(jax.S...  19.6 us
    pallas_call x1, Pallas kernels, placed(): pl.pallas_call(place_kernel, out_shape=jax.ShapeDtypeStruct((rows, groups...  10.6 us
  transfers between devices with their start and end apart: 1, of which 0 were waited for; matrix products, arithmetic and copies ran while one was open for 0% of the time, Pallas kernels for 42%

profile of v2, /device:TPU:1, one launch (start us, length us, event | category | flops | bytes accessed | tf_op | source)
XLA Modules:
  0.0 209.0 jit_solution(12402404096304356502)
XLA Ops:
  7.2 0.0 all-gather.3.cloned.1.call-start
  7.2 60.2 %swap.1 = (f32[8,64,8,256]{3,2,1,0:T(8,128)}, f32[8,64,256]{2,1,0:T(8,128)}) custom-call(f32[64,64,256]{2,1,0:T(8,128)} %x_ref.1, f32[64,256]{1,0:T(8,128)} %f_ref.1), custom_call_target="tpu_custom_call" | custom-call | tf_op jit(solution)/shard_map/swap/pallas_call | solution.py:92
  67.4 2.1 copy.8
  69.5 0.0 copy-start
  69.5 0.0 copy-start.1
  69.5 19.6 %products.1 = (f32[512,512]{1,0:T(8,128)}, f32[8,256,256]{2,1,0:T(8,128)}) custom-call(f32[8,64,8,256]{3,2,1,0:T(8,128)} %get-tuple-element.7.x_ref, f32[256,512]{1,0:T(8,128)} %bitcast.5), custom_call_target="tpu_custom_call" | custom-call | tf_op jit(solution)/shard_map/products/pallas_call | solution.py:138
  89.1 21.3 %all_to_all.5 = f32[8,64,512]{2,1,0:T(8,128)S(1)} all-to-all(f32[8,64,512]{2,1,0:T(8,128)} %bitcast.6), channel_id=1, replica_groups=mesh['xy'=32,'gz'=8] {'gz'}, dimensions={0} | all-to-all | bytes 2097152 | tf_op jit(solution)/shard_map/all_to_all | solution.py:268
  110.4 0.7 reduce_sum.18
  111.1 0.0 all-gather.3.cloned.1.call-update
  111.1 0.0 copy-done
  111.1 0.0 copy-done.1
  111.1 0.6 and_select_fusion
  111.8 76.7 %scatter.1.in_ref = f32[3,8,8,32,256]{4,3,2,1,0:T(8,128)} custom-call(f32[8,256,256]{2,1,0:T(8,128)} %get-tuple-element.11.core_ref), custom_call_target="tpu_custom_call" | custom-call | bytes 200000000 | tf_op jit(solution)/shard_map/scatter/pallas_call | solution.py:211
  188.4 10.6 %placed.1 = f32[32,64,256]{2,1,0:T(8,128)} custom-call(s32[2]{0:T(128)} %get-tuple-element.13.which_ref, s32[2]{0:T(128)} %get-tuple-element.12.half_ref, f32[3,8,8,32,256]{4,3,2,1,0:T(8,128)} %scatter.1.in_ref), custom_call_target="tpu_custom_call" | custom-call | tf_op jit(solution)/shard_map/placed/pallas_call | solution.py:247
  199.0 0.0 all-gather.3.cloned.1.call-done
  199.0 3.2 %reduce_sum.19 = f32[64,512]{1,0:T(8,128)} reduce(f32[32,64,512]{2,1,0:T(8,128)} %bitcast.4, f32[]{:T(128)} %constant.29.clone.1), dimensions={0}, to_apply=%region_1.2 | reduce | flops 1015808 | bytes 4325380 | tf_op jit(solution)/shard_map/reduce_sum | solution.py:271
Async XLA Ops:
  7.2 191.8 %all-gather.3.cloned.1.call-start = ((), (), s32[]{:S(2)}) async-start(), calls=%async_computation.1 | async-start | bytes 4325376 | tf_op jit(solution)/shard_map/all_gather | solution.py:271
  69.5 41.6 %copy-start = (s32[64]{0:T(128)S(1)}, s32[64]{0:T(128)}, u32[]{:S(2)}) copy-start(s32[64]{0:T(128)} %param.7) | copy-start | bytes 772
  69.5 41.7 %copy-start.1 = (s32[64]{0:T(128)S(1)}, s32[64]{0:T(128)}, u32[]{:S(2)}) copy-start(s32[64]{0:T(128)} %param.6) | copy-start | bytes 772
Sparse Core Ops, SparseCore 0:
  111.2 79.8 all-gather.2
